TPU v7x, 256 devices: a whole 4x4x8 slice. The times are simulated.
256 devices in a mesh: ctx: 16 (over y_lo, x, core), chan: 16 (over z, y_hi).
Axes of the slice: x: 4, y: 4 (y_hi: 2, y_lo: 2; y = y_hi * 2 + y_lo), z: 8, core: 2. Of those that a mesh axis runs over, the one named last changes fastest.
Arguments:
- features: bfloat16 [3, 4096, 4096], P(None, 'ctx', 'chan'), may hold values from -6 to 6
- saved_conv: bfloat16 [4096, 4096], P('ctx', 'chan'), may hold values from -6 to 6
- grad_out: bfloat16 [4096, 4096], P('ctx', 'chan'), may hold values from -6 to 6
- out_weight: bfloat16 [4096, 4096], P('chan'), may hold values from -0.09375 to 0.09375
- in_weight: bfloat16 [3, 4096, 4096], P(None, None, 'chan'), may hold values from -0.09375 to 0.09375
- short_taps: float32 [3, 3, 4096], P(None, None, 'chan'), may hold values from -3.5 to 3.5
- residues: float32 [16, 4096], P(None, 'chan'), may hold values from -1 to 1
- decay_time: float32 [16, 4096], P(None, 'chan'), may hold values from 25 to 20480
Outputs:
- grad_input: bfloat16 [4096, 4096], P('chan', 'ctx')
- grad_residue: float32 [16, 4096], P(None, 'chan')
All inputs are finite; a program needn't handle non-finite values.
Results may differ from a plain program's by a relative error of at most 0.019.
Values may be sent and summed in bfloat16 or wider, within the bound.
A program may use at most 64 MiB of HBM per device.

v0:
```python
import jax
import jax.numpy as jnp
from jax import lax
from jax.sharding import PartitionSpec as P


def passed_along(value, axis, steps):
    count = lax.axis_size(axis)
    leading, last = (max(0, -steps), min(count, count - steps))
    return lax.ppermute(value, axis, [(source, source + steps) for source in range(leading, last)])


def local(features, saved_conv, grad_out, out_weight, in_weight, short_taps, residues, decay_time):
    highest = lax.Precision.HIGHEST
    length = features.shape[1]
    width = features.shape[2]
    poles = residues.shape[0]
    taps = short_taps.shape[1]
    span_rows = 128
    blocks = length // span_rows
    query_act = features[0].astype(jnp.float32)
    key_act = features[1].astype(jnp.float32)
    value_act = features[2].astype(jnp.float32)
    contract = (((1,), (1,)), ((), ()))
    everything = lax.all_gather(grad_out, "chan", axis=1, tiled=True)
    grad_gate = lax.dot_general(
        everything, out_weight, contract, preferred_element_type=jnp.float32
    )
    grad_conv = grad_gate * query_act
    grad_query = grad_gate * saved_conv.astype(jnp.float32)
    product = key_act * value_act
    rate = 1.0 / decay_time
    offset = jnp.arange(span_rows, dtype=jnp.float32)
    falling = jnp.exp(-rate[None] * offset[:, None, None])
    rising = jnp.exp(rate[None] * offset[:, None, None])
    closing = jnp.exp(-rate[None] * (span_rows - offset)[:, None, None])
    weighted = grad_conv.reshape(blocks, span_rows, 1, width) * falling[None]
    upper = (offset[None, :] >= offset[:, None]).astype(jnp.float32)
    tails = jnp.einsum(
        "st,btx->bsx",
        upper,
        weighted.reshape(blocks, span_rows, poles * width),
        precision=highest,
        preferred_element_type=jnp.float32,
    )
    tails = tails.reshape(blocks, span_rows, poles, width)
    starts = tails[:, 0]
    order = jnp.arange(blocks)
    gap = order[None, :] - order[:, None] - 1
    distance = (span_rows * jnp.maximum(gap, 0)).astype(jnp.float32)
    factor = jnp.where(
        gap[:, :, None, None] >= 0, jnp.exp(-rate[None, None] * distance[:, :, None, None]), 0.0
    )
    beyond = jnp.sum(factor * starts[None], axis=1)
    block_span = jnp.exp(-rate * span_rows)
    own_start = starts[0] + block_span * beyond[0]
    device_span = jnp.exp(-rate * length)
    empty = jnp.zeros_like(rate)

    def relay(step, incoming):
        return passed_along(own_start + device_span * incoming, "ctx", -1)

    incoming = lax.fori_loop(0, lax.axis_size("ctx") - 1, relay, empty)
    remain = (blocks - 1 - order).astype(jnp.float32)
    entering = beyond + jnp.exp(-rate[None] * span_rows * remain[:, None, None]) * incoming[None]
    state = tails * rising[None] + closing[None] * entering[:, None]
    grad_product = jnp.sum(residues[None, None] * state, axis=2).reshape(length, width)
    partial_res = jnp.sum(product.reshape(blocks, span_rows, 1, width) * state, axis=(0, 1))
    grad_key = grad_product * value_act
    grad_value = grad_product * key_act
    grad_acts = jnp.stack([grad_query, grad_key, grad_value])
    after = passed_along(grad_acts[:, : taps - 1, :], "ctx", -1)
    extended = jnp.concatenate([grad_acts, after], axis=1)
    filtered = short_taps[:, 0, None, :] * extended[:, 0:length, :]
    for lag in range(1, taps):
        filtered = filtered + short_taps[:, lag, None, :] * extended[:, lag : lag + length, :]
    grad_proj = filtered.astype(jnp.bfloat16)
    grad_input = lax.psum_scatter(
        jnp.einsum("jdc,jtc->dt", in_weight, grad_proj, preferred_element_type=jnp.float32).astype(
            jnp.bfloat16
        ),
        "chan",
        scatter_dimension=0,
        tiled=True,
    )
    grad_residue = lax.psum(partial_res, "ctx") / (length * lax.axis_size("ctx"))
    return (grad_input, grad_residue)


def solution(mesh):
    return jax.shard_map(
        local,
        mesh=mesh,
        in_specs=(
            P(None, "ctx", "chan"),
            P("ctx", "chan"),
            P("ctx", "chan"),
            P("chan", None),
            P(None, None, "chan"),
            P(None, None, "chan"),
            P(None, "chan"),
            P(None, "chan"),
        ),
        out_specs=(P("chan", "ctx"), P(None, "chan")),
        check_vma=False,
    )
```

profile of v0, /device:TPU:32, one launch (start us, length us, event | category | flops | bytes accessed | tf_op | source)
XLA Modules:
  0.0 449.0 jit_solution(12016435469168271515)
XLA Ops:
  7.2 0.7 all-gather.2.cloned.1.call-update
  7.9 0.0 reduce-scatter.2.cloned.1.call-start
  8.0 0.7 fusion.18
  8.8 0.8 fusion.20
  9.6 3.1 multiply_exponential_fusion.2
  12.7 2.3 multiply_exponential_fusion
  15.1 82.5 %all-gather.2.cloned.1.call-done = bf16[256,4096]{1,0:T(8,128)(2,1)} async-done(((bf16[256,256]{1,0:T(8,128)(2,1)}), bf16[256,4096]{1,0:T(8,128)(2,1)}) %all-gather.2.cloned.1.call-update) | async-done | bytes 2097168 | tf_op jit(solution)/shard_map/all_gather | solution.py:25
  97.6 2.3 multiply_bitcast_fusion
  100.0 0.1 copy.25
  100.1 1.9 bitcast_multiply_fusion.2
  102.0 2.1 fusion.12
  104.1 1.6 slice.51
  105.7 1.0 copy-done.1
  106.7 2.8 copy.34
  109.6 2.2 copy.35
  111.8 0.1 multiply_reduce_fusion.1
  111.9 78.9 %while.10 = (s32[]{:T(128)}, f32[16,256]{1,0:T(8,128)S(1)}, f32[16,256]{1,0:T(8,128)S(1)}, f32[16,256]{1,0:T(8,128)S(1)}, s32[]{:T(128)}) while((s32[]{:T(128)}, f32[16,256]{1,0:T(8,128)S(1)}, f32[16,256]{1,0:T(8,128)S(1)}, f32[16,256]{1,0:T(8,128)S(1)}, s32[]{:T(128)}) %tuple.40), condition=%wide.region_2.3_spmd, body=%wide.region_1.2_spmd.sunk | while | flops 8194 | bytes 131173 | solution.py:63
  112.0 1.3 collective-permute-start
  113.3 1.8 collective-permute-done
  115.0 1.3 collective-permute-start
  116.3 3.1 collective-permute-done
  119.4 1.3 collective-permute-start
  120.7 3.8 collective-permute-done
  124.5 1.3 collective-permute-start
  125.8 3.8 collective-permute-done
  129.5 1.3 collective-permute-start
  130.8 3.8 collective-permute-done
  134.6 1.3 collective-permute-start
  135.9 3.8 collective-permute-done
  139.7 1.3 collective-permute-start
  140.9 3.8 collective-permute-done
  144.7 1.3 collective-permute-start
  146.0 3.8 collective-permute-done
  149.8 1.3 collective-permute-start
  151.0 3.8 collective-permute-done
  154.8 1.3 collective-permute-start
  156.1 3.8 collective-permute-done
  159.9 1.3 collective-permute-start
  161.2 3.8 collective-permute-done
  164.9 1.3 collective-permute-start
  166.2 3.8 collective-permute-done
  170.0 1.3 collective-permute-start
  171.3 5.2 %collective-permute-done = f32[16,256]{1,0:T(8,128)S(1)} collective-permute-done((f32[16,256]{1,0:T(8,128)S(1)}, f32[16,256]{1,0:T(8,128)S(1)}, u32[]{:S(2)}, u32[]{:S(2)}) %collective-permute-start) | collective-permute-done | bytes 16416 | tf_op jit(solution)/shard_map/while/body/eval_jaxpr/ppermute | solution.py:10
  176.5 1.3 collective-permute-start
  177.8 5.9 %collective-permute-done = f32[16,256]{1,0:T(8,128)S(1)} collective-permute-done((f32[16,256]{1,0:T(8,128)S(1)}, f32[16,256]{1,0:T(8,128)S(1)}, u32[]{:S(2)}, u32[]{:S(2)}) %collective-permute-start) | collective-permute-done | bytes 16416 | tf_op jit(solution)/shard_map/while/body/eval_jaxpr/ppermute | solution.py:10
  183.7 1.3 collective-permute-start
  185.0 5.9 %collective-permute-done = f32[16,256]{1,0:T(8,128)S(1)} collective-permute-done((f32[16,256]{1,0:T(8,128)S(1)}, f32[16,256]{1,0:T(8,128)S(1)}, u32[]{:S(2)}, u32[]{:S(2)}) %collective-permute-start) | collective-permute-done | bytes 16416 | tf_op jit(solution)/shard_map/while/body/eval_jaxpr/ppermute | solution.py:10
  190.8 0.1 multiply_add_fusion.2
  190.9 4.9 %multiply_reduce_fusion = f32[2,128,256]{1,2,0:T(8,128)S(1)} fusion(f32[2,128,16,256]{1,3,2,0:T(8,128)} %bitcast.72, f32[2,16,256]{2,1,0:T(8,128)S(1)} %multiply_add_fusion.2, f32[128,16,256]{0,2,1:T(8,128)} %get-tuple-element.58, f32[128,16,256]{0,2,1:T(8,128)} %get-tuple-element.59, f32[16,256]{1,0:T(8,128)S(1)} %copy-done.5), kind=kLoop, calls=%fused_computation.9 | loop fusion | flops 5177344 | bytes 8699904 | tf_op jit(solution)/shard_map/reduce_sum | solution.py:67
  195.8 0.1 copy.28
  195.9 0.1 convert_multiply_fusion.2
  196.0 0.1 pad_maximum_fusion.1
  196.1 1.3 collective-permute-start.1
  197.4 5.8 %collective-permute-done.1 = f32[3,2,256]{2,1,0:T(2,128)S(1)} collective-permute-done((f32[3,2,256]{2,1,0:T(2,128)S(1)}, f32[3,2,256]{2,1,0:T(2,128)S(1)}, u32[]{:S(2)}, u32[]{:S(2)}) %collective-permute-start.1) | collective-permute-done | bytes 6176 | tf_op jit(solution)/shard_map/ppermute | solution.py:10
  203.2 0.1 pad_maximum_fusion
  203.3 6.0 %fusion.1 = bf16[4096,256]{0,1:T(8,128)(2,1)} fusion(bf16[3,4096,256]{2,1,0:T(8,128)(2,1)} %param.14, f32[3,258,256]{2,1,0:T(8,128)S(1)} %pad_maximum_fusion, f32[3,256]{1,0:T(4,128)S(1)} %get-tuple-element.60, f32[3,256]{1,0:T(4,128)S(1)} %get-tuple-element.61, f32[3,256]{1,0:T(4,128)S(1)} %bitcast.84, f32[1,256,256]{2,1,0:T(8,128)S(1)} %get-tuple-element.42, ...), kind=kOutput, calls=%fused_computation.3 | convolution fusion | flops 1613234176 | bytes 10760192 | tf_op jit(solution)/shard_map/jdc,jtc->dt/dot_general | solution.py:79
  209.4 1.7 multiply_exponential_fusion.1
  211.1 0.1 copy.29
  211.3 0.1 multiply_add_fusion.1
  211.4 4.4 fusion.2
  215.8 69.7 %psum.7 = f32[16,256]{1,0:T(8,128)S(1)} all-reduce(f32[16,256]{1,0:T(8,128)S(1)} %reduce_sum.35), channel_id=1, replica_groups=mesh['ctx'=16,'chan'=16] {'ctx'}, use_global_device_ids=true, to_apply=%region_6.7 | all-reduce | flops 4096 | bytes 32768 | tf_op jit(solution)/shard_map/psum | solution.py:86
  285.5 0.6 broadcast_multiply_fusion
  286.1 154.4 %reduce-scatter.2.cloned.1.call-done = bf16[256,256]{0,1:T(8,128)(2,1)} async-done(((bf16[4096,256]{0,1:T(8,128)(2,1)}), bf16[256,256]{0,1:T(8,128)(2,1)}) %reduce-scatter.2.cloned.1.call-update) | async-done | bytes 131088 | tf_op jit(solution)/shard_map/reduce_scatter | solution.py:78
  440.5 1.7 copy.30
  (43 shorter events, 0.3 us)
Async XLA Ops:
  7.2 90.5 %copy-start = (bf16[256,4096]{1,0:T(8,128)(2,1)S(1)}, bf16[256,4096]{1,0:T(8,128)(2,1)}, u32[]{:S(2)}) copy-start(bf16[256,4096]{1,0:T(8,128)(2,1)} %param.13) | copy-start | bytes 6291460
  7.2 90.4 %all-gather.2.cloned.1.call-start = ((), (), s32[]{:S(2)}) async-start(), calls=%async_computation.1 | async-start | bytes 2228224 | tf_op jit(solution)/shard_map/all_gather | solution.py:25
  7.9 432.6 %reduce-scatter.2.cloned.1.call-start = ((), (), s32[]{:S(2)}) async-start(), calls=%async_computation.2 | async-start | bytes 2228224 | tf_op jit(solution)/shard_map/reduce_scatter | solution.py:78
  12.7 84.9 %copy-start.2 = (bf16[3,256,256]{2,1,0:T(8,128)(2,1)S(1)}, bf16[3,256,256]{2,1,0:T(8,128)(2,1)}, u32[]{:S(2)}) copy-start(bf16[3,256,256]{2,1,0:T(8,128)(2,1)} %param.10) | copy-start | bytes 1179652
  12.7 84.9 %copy-start.3 = (bf16[256,256]{1,0:T(8,128)(2,1)S(1)}, bf16[256,256]{1,0:T(8,128)(2,1)}, u32[]{:S(2)}) copy-start(bf16[256,256]{1,0:T(8,128)(2,1)} %param.11) | copy-start | bytes 393220
  104.1 2.6 copy-start.1
  109.5 2.3 copy-start.4
  109.5 81.4 %copy-start.5 = (f32[16,256]{1,0:T(8,128)S(1)}, f32[16,256]{1,0:T(8,128)}, u32[]{:S(2)}) copy-start(f32[16,256]{1,0:T(8,128)} %param.16) | copy-start | bytes 49156
  112.0 3.1 collective-permute-start
  115.0 4.4 collective-permute-start
  119.4 5.0 %collective-permute-start = (f32[16,256]{1,0:T(8,128)S(1)}, f32[16,256]{1,0:T(8,128)S(1)}, u32[]{:S(2)}, u32[]{:S(2)}) collective-permute-start(f32[16,256]{1,0:T(8,128)S(1)} %multiply_add_fusion.4), channel_id=1, source_target_pairs={{16,0},{32,16},{48,32},{64,48},{80,64},{96,80},{112,96},{128,112},... | collective-permute-start | bytes 49160 | tf_op jit(solution)/shard_map/while/body/eval_jaxpr/ppermute | solution.py:10
  124.5 5.0 %collective-permute-start = (f32[16,256]{1,0:T(8,128)S(1)}, f32[16,256]{1,0:T(8,128)S(1)}, u32[]{:S(2)}, u32[]{:S(2)}) collective-permute-start(f32[16,256]{1,0:T(8,128)S(1)} %multiply_add_fusion.4), channel_id=1, source_target_pairs={{16,0},{32,16},{48,32},{64,48},{80,64},{96,80},{112,96},{128,112},... | collective-permute-start | bytes 49160 | tf_op jit(solution)/shard_map/while/body/eval_jaxpr/ppermute | solution.py:10
  129.5 5.0 %collective-permute-start = (f32[16,256]{1,0:T(8,128)S(1)}, f32[16,256]{1,0:T(8,128)S(1)}, u32[]{:S(2)}, u32[]{:S(2)}) collective-permute-start(f32[16,256]{1,0:T(8,128)S(1)} %multiply_add_fusion.4), channel_id=1, source_target_pairs={{16,0},{32,16},{48,32},{64,48},{80,64},{96,80},{112,96},{128,112},... | collective-permute-start | bytes 49160 | tf_op jit(solution)/shard_map/while/body/eval_jaxpr/ppermute | solution.py:10
  134.6 5.0 %collective-permute-start = (f32[16,256]{1,0:T(8,128)S(1)}, f32[16,256]{1,0:T(8,128)S(1)}, u32[]{:S(2)}, u32[]{:S(2)}) collective-permute-start(f32[16,256]{1,0:T(8,128)S(1)} %multiply_add_fusion.4), channel_id=1, source_target_pairs={{16,0},{32,16},{48,32},{64,48},{80,64},{96,80},{112,96},{128,112},... | collective-permute-start | bytes 49160 | tf_op jit(solution)/shard_map/while/body/eval_jaxpr/ppermute | solution.py:10
  139.7 5.0 %collective-permute-start = (f32[16,256]{1,0:T(8,128)S(1)}, f32[16,256]{1,0:T(8,128)S(1)}, u32[]{:S(2)}, u32[]{:S(2)}) collective-permute-start(f32[16,256]{1,0:T(8,128)S(1)} %multiply_add_fusion.4), channel_id=1, source_target_pairs={{16,0},{32,16},{48,32},{64,48},{80,64},{96,80},{112,96},{128,112},... | collective-permute-start | bytes 49160 | tf_op jit(solution)/shard_map/while/body/eval_jaxpr/ppermute | solution.py:10
  144.7 5.0 %collective-permute-start = (f32[16,256]{1,0:T(8,128)S(1)}, f32[16,256]{1,0:T(8,128)S(1)}, u32[]{:S(2)}, u32[]{:S(2)}) collective-permute-start(f32[16,256]{1,0:T(8,128)S(1)} %multiply_add_fusion.4), channel_id=1, source_target_pairs={{16,0},{32,16},{48,32},{64,48},{80,64},{96,80},{112,96},{128,112},... | collective-permute-start | bytes 49160 | tf_op jit(solution)/shard_map/while/body/eval_jaxpr/ppermute | solution.py:10
  149.8 5.0 %collective-permute-start = (f32[16,256]{1,0:T(8,128)S(1)}, f32[16,256]{1,0:T(8,128)S(1)}, u32[]{:S(2)}, u32[]{:S(2)}) collective-permute-start(f32[16,256]{1,0:T(8,128)S(1)} %multiply_add_fusion.4), channel_id=1, source_target_pairs={{16,0},{32,16},{48,32},{64,48},{80,64},{96,80},{112,96},{128,112},... | collective-permute-start | bytes 49160 | tf_op jit(solution)/shard_map/while/body/eval_jaxpr/ppermute | solution.py:10
  154.8 5.0 %collective-permute-start = (f32[16,256]{1,0:T(8,128)S(1)}, f32[16,256]{1,0:T(8,128)S(1)}, u32[]{:S(2)}, u32[]{:S(2)}) collective-permute-start(f32[16,256]{1,0:T(8,128)S(1)} %multiply_add_fusion.4), channel_id=1, source_target_pairs={{16,0},{32,16},{48,32},{64,48},{80,64},{96,80},{112,96},{128,112},... | collective-permute-start | bytes 49160 | tf_op jit(solution)/shard_map/while/body/eval_jaxpr/ppermute | solution.py:10
  159.9 5.0 %collective-permute-start = (f32[16,256]{1,0:T(8,128)S(1)}, f32[16,256]{1,0:T(8,128)S(1)}, u32[]{:S(2)}, u32[]{:S(2)}) collective-permute-start(f32[16,256]{1,0:T(8,128)S(1)} %multiply_add_fusion.4), channel_id=1, source_target_pairs={{16,0},{32,16},{48,32},{64,48},{80,64},{96,80},{112,96},{128,112},... | collective-permute-start | bytes 49160 | tf_op jit(solution)/shard_map/while/body/eval_jaxpr/ppermute | solution.py:10
  164.9 5.0 %collective-permute-start = (f32[16,256]{1,0:T(8,128)S(1)}, f32[16,256]{1,0:T(8,128)S(1)}, u32[]{:S(2)}, u32[]{:S(2)}) collective-permute-start(f32[16,256]{1,0:T(8,128)S(1)} %multiply_add_fusion.4), channel_id=1, source_target_pairs={{16,0},{32,16},{48,32},{64,48},{80,64},{96,80},{112,96},{128,112},... | collective-permute-start | bytes 49160 | tf_op jit(solution)/shard_map/while/body/eval_jaxpr/ppermute | solution.py:10
  170.0 6.5 %collective-permute-start = (f32[16,256]{1,0:T(8,128)S(1)}, f32[16,256]{1,0:T(8,128)S(1)}, u32[]{:S(2)}, u32[]{:S(2)}) collective-permute-start(f32[16,256]{1,0:T(8,128)S(1)} %multiply_add_fusion.4), channel_id=1, source_target_pairs={{16,0},{32,16},{48,32},{64,48},{80,64},{96,80},{112,96},{128,112},... | collective-permute-start | bytes 49160 | tf_op jit(solution)/shard_map/while/body/eval_jaxpr/ppermute | solution.py:10
  176.5 7.2 %collective-permute-start = (f32[16,256]{1,0:T(8,128)S(1)}, f32[16,256]{1,0:T(8,128)S(1)}, u32[]{:S(2)}, u32[]{:S(2)}) collective-permute-start(f32[16,256]{1,0:T(8,128)S(1)} %multiply_add_fusion.4), channel_id=1, source_target_pairs={{16,0},{32,16},{48,32},{64,48},{80,64},{96,80},{112,96},{128,112},... | collective-permute-start | bytes 49160 | tf_op jit(solution)/shard_map/while/body/eval_jaxpr/ppermute | solution.py:10
  183.7 7.2 %collective-permute-start = (f32[16,256]{1,0:T(8,128)S(1)}, f32[16,256]{1,0:T(8,128)S(1)}, u32[]{:S(2)}, u32[]{:S(2)}) collective-permute-start(f32[16,256]{1,0:T(8,128)S(1)} %multiply_add_fusion.4), channel_id=1, source_target_pairs={{16,0},{32,16},{48,32},{64,48},{80,64},{96,80},{112,96},{128,112},... | collective-permute-start | bytes 49160 | tf_op jit(solution)/shard_map/while/body/eval_jaxpr/ppermute | solution.py:10
  196.1 7.2 %collective-permute-start.1 = (f32[3,2,256]{2,1,0:T(2,128)S(1)}, f32[3,2,256]{2,1,0:T(2,128)S(1)}, u32[]{:S(2)}, u32[]{:S(2)}) collective-permute-start(f32[3,2,256]{2,1,0:T(2,128)S(1)} %slice.53), channel_id=1, source_target_pairs={{16,0},{32,16},{48,32},{64,48},{80,64},{96,80},{112,96},{128,112},... | collective-permute-start | bytes 18440 | tf_op jit(solution)/shard_map/ppermute | solution.py:10
Sparse Core Ops, SparseCore 0:
  10.5 87.1 all-gather.1
  209.4 230.9 reduce-scatter.1
where the time goes:
time: 451 us; the launch traced here: 449 us
  waiting for transfers between devices  303 us (67%)
  blocking collectives  69.7 us (15%)
  starting transfers between devices  20.6 us (5%)
  other arithmetic  20.2 us (4%)
  between operations  14.3 us (3%)
  local copies, waits for them, and re-layouts  10.6 us (2%)
  matrix products  10.5 us (2%)
    reduce_scatter x1, waiting for transfers between devices, local(): lax.psum_scatter(jnp.einsum('jdc,jtc->dt', in_weight, grad_proj, preferre...  154 us
    all_gather x1, waiting for transfers between devices, local(): everything = lax.all_gather(grad_out, 'chan', axis=1, tiled=True)  82.5 us
    psum x1, blocking collectives, local(): lax.psum(partial_res, 'ctx') / (length * lax.axis_size('ctx'))  69.7 us
    ppermute x16, waiting for transfers between devices, passed_along(): lax.ppermute(value, axis, [(source, source + steps) for source in range(l...  65.2 us
    ppermute x16, starting transfers between devices, passed_along(): lax.ppermute(value, axis, [(source, source + steps) for source in range(l...  20.5 us
  transfers between devices with their start and end apart: 18, of which 18 were waited for; matrix products, arithmetic and copies ran while one was open for 3% of the time, Pallas kernels for 0%

commit v1 on v0

v1 whole, which is shorter than its diff:
```python
import functools

import jax
import jax.numpy as jnp
from jax import lax
from jax.experimental import pallas as pl
from jax.experimental.pallas import tpu as pltpu
from jax.sharding import PartitionSpec as P

MESH = pl.DeviceIdType.MESH
F32 = jnp.float32
BF16 = jnp.bfloat16
NT = (((1,), (1,)), ((), ()))
CHAINS = 4


def kernel(
    go, feat, conv, ow, iw, taps, res, decay,
    out, gres,
    blocks, owv, iwv, fv, cv, tv, rv, dv,
    acc, grow, prod, acts, gp, gprod, lam_ref, ent, csum,
    sown, sin, hsend, hrecv, kvh, rown, rin,
    part, tx, rx, ysend, yrecv,
    in_sem, ag_s, ag_r, agy_s, agy_r, kv_s, kv_r, h_s, h_r,
    s_s, s_r, r_s, r_r, rs_s, rs_r, rsy_s, rsy_r,
):
    n_ctx = lax.axis_size("ctx")
    n_z = lax.axis_size("chan") // 2
    me = lax.axis_index("ctx")
    ch = lax.axis_index("chan")
    z = ch // 2
    yh = lax.rem(ch, 2)
    length = acc.shape[0]
    half_rows = length // 2

    def chan_of(zz, yy):
        return lax.rem(zz + 2 * n_z, n_z) * 2 + yy

    partner = chan_of(z, 1 - yh)
    sides = [chan_of(z + 1, yh), chan_of(z - 1, yh)]
    dirs = (1, -1)

    pairs = [(go, blocks.at[ch]), (ow, owv), (feat, fv), (conv, cv), (taps, tv),
             (res, rv), (decay, dv), (iw, iwv)]
    local = [pltpu.make_async_copy(a, b, in_sem.at[i]) for i, (a, b) in enumerate(pairs)]
    for c in local:
        c.start()

    barrier = pltpu.get_barrier_semaphore()
    for dst in (sides[0], sides[1], partner):
        pl.semaphore_signal(barrier, inc=1, device_id={"chan": dst}, device_id_type=MESH)
    for k in range(1, n_ctx):
        pl.semaphore_signal(
            barrier, inc=1, device_id={"ctx": lax.rem(me + k, n_ctx)}, device_id_type=MESH
        )
    pl.semaphore_wait(barrier, 3 + n_ctx - 1)

    def remote(src, dst, ss, rs, **where):
        return pltpu.make_async_remote_copy(
            src_ref=src, dst_ref=dst, send_sem=ss, recv_sem=rs,
            device_id=where, device_id_type=MESH,
        )

    def rows(half):
        return pl.ds(half * half_rows, half_rows)

    def ag(d, q, h, half, receiving=False):
        slot = (2 * h + half) if h < 3 else 6
        source = z - dirs[d] * (h + (1 if receiving else 0))
        block = chan_of(source, yh if q == 0 else 1 - yh)
        ref = blocks.at[block, rows(half)]
        src = go.at[rows(half)] if (q == 0 and h == 0 and not receiving) else ref
        return remote(src, ref, ag_s.at[d, q, slot], ag_r.at[d, q, slot], chan=sides[d])

    def agy(half, receiving=False):
        ref = blocks.at[partner if receiving else ch, rows(half)]
        src = ref if receiving else go.at[rows(half)]
        return remote(src, ref, agy_s.at[half], agy_r.at[half], chan=partner)

    sent = []

    def send(c):
        c.start()
        sent.append(c)

    for half in range(2):
        for d in range(2):
            send(ag(d, 0, 0, half))
        send(agy(half))

    prev = lax.rem(me + n_ctx - 1, n_ctx)

    @pl.when(me > 0)
    def _():
        remote(feat.at[pl.ds(1, 2), pl.ds(0, 16)], kvh, kv_s.at[0], kv_r.at[0], ctx=prev).start()

    @pl.when(me == n_ctx - 1)
    def _():
        kvh[...] = jnp.zeros_like(kvh)
        hrecv[...] = jnp.zeros_like(hrecv)

    first = [True]

    def multiply(block):
        cols = pl.ds(pl.multiple_of(block * length, length), length)
        term = lax.dot_general(blocks[block], owv[:, cols], NT, preferred_element_type=F32)
        if first[0]:
            acc[...] = term
            first[0] = False
        else:
            acc[...] += term

    local[0].wait()
    local[1].wait()
    multiply(ch)
    for q in range(2):
        other = yh if q == 0 else 1 - yh
        if q == 1:
            for half in range(2):
                agy(half, True).wait_recv()
                for d in range(2):
                    send(ag(d, 1, 0, half))
            multiply(partner)
        for h in range(1, 4):
            for half in range(2):
                for d in range(2):
                    ag(d, q, h - 1, half, True).wait_recv()
                    if h < 3 or half == d:
                        send(ag(d, q, h, half))
            multiply(chan_of(z - h, other))
            multiply(chan_of(z + h, other))
        if q == 0:
            for i in range(2, 7):
                local[i].wait()
            rate = 1.0 / dv[...]
            lam_ref[0] = jnp.exp(-rate)
            lam_ref[1] = jnp.exp(-rate * (length // CHAINS))
            lam_ref[2] = jnp.exp(-rate * length)
            lam_ref[3] = jnp.exp(rate)
            prod[...] = fv[1].astype(F32) * fv[2].astype(F32)
        for d in range(2):
            ag(d, q, 3, d, True).wait_recv()
        multiply(chan_of(z + n_z // 2, other))

    gate = acc[...]
    grow[...] = gate * fv[0].astype(F32)
    acts[0, pl.ds(0, length)] = gate * cv[...].astype(F32)

    @pl.when(me > 0)
    def _():
        hsend[pl.ds(0, 8)] = acts[0, pl.ds(0, 8)]
        hsend[pl.ds(8, 8)] = grow[pl.ds(0, 8)]
        remote(hsend, hrecv, h_s.at[0], h_r.at[0], ctx=prev).start()

    run = length // CHAINS
    lam = lam_ref[0]

    def sum_step(i, carry):
        fresh = []
        for k in range(CHAINS):
            g = grow[pl.ds(k * run + run - 1 - i, 1)]
            fresh.append(g + lam * carry[k])
        return tuple(fresh)

    zero = jnp.zeros_like(lam)
    sums = lax.fori_loop(0, run, sum_step, (zero,) * CHAINS, unroll=8)
    total = sums[CHAINS - 1]
    for k in range(CHAINS - 2, -1, -1):
        total = sums[k] + lam_ref[1] * total
    for k in range(CHAINS):
        csum[k] = sums[k]
    sown[...] = total

    for k in range(1, n_ctx):
        @pl.when(me >= k)
        def _():
            dst = lax.rem(me + n_ctx - k, n_ctx)
            remote(sown, sin.at[me], s_s.at[k], s_r.at[me], ctx=dst).start()

    @pl.when(me < n_ctx - 1)
    def _():
        nxt = lax.rem(me + 1, n_ctx)
        remote(hsend, hrecv, h_s.at[0], h_r.at[0], ctx=nxt).wait_recv()
        remote(feat.at[pl.ds(1, 2), pl.ds(0, 16)], kvh, kv_s.at[0], kv_r.at[0], ctx=nxt).wait_recv()

    acts[0, pl.ds(length, 8)] = hrecv[pl.ds(0, 8)]

    def short(i):
        y = tv[i, pl.ds(0, 1)] * acts[i, pl.ds(0, length)]
        y = y + tv[i, pl.ds(1, 1)] * acts[i, pl.ds(1, length)]
        y = y + tv[i, pl.ds(2, 1)] * acts[i, pl.ds(2, length)]
        gp[i] = y.astype(BF16)

    short(0)

    ent[...] = jnp.zeros_like(ent)
    for j in range(n_ctx - 1, 0, -1):
        @pl.when(j > me)
        def _():
            remote(sown, sin.at[j], s_s.at[0], s_r.at[j], ctx=j).wait_recv()
            ent[...] = sin[j] + lam_ref[2] * ent[...]

    entering = ent[...]
    residue = rv[...]
    starts = [None] * CHAINS
    starts[CHAINS - 1] = entering
    for k in range(CHAINS - 2, -1, -1):
        starts[k] = csum[k + 1] + lam_ref[1] * starts[k + 1]

    def full_step(i, carry):
        states, totals = carry
        fresh, summed = [], []
        for k in range(CHAINS):
            r = k * run + run - 1 - i
            s = grow[pl.ds(r, 1)] + lam * states[k]
            gprod[pl.ds(r, 1)] = jnp.sum(residue * s, axis=0, keepdims=True)
            totals = totals + prod[pl.ds(r, 1)] * s
            fresh.append(s)
        return tuple(fresh), totals

    _, totals = lax.fori_loop(0, run, full_step, (tuple(starts), zero), unroll=4)
    rown[...] = totals
    beyond = (entering - hrecv[pl.ds(8, 1)]) * lam_ref[3]
    gprod[pl.ds(length, 1)] = jnp.sum(residue * entering, axis=0, keepdims=True)
    gprod[pl.ds(length + 1, 1)] = jnp.sum(residue * beyond, axis=0, keepdims=True)
    acts[1, pl.ds(0, length)] = gprod[pl.ds(0, length)] * fv[2].astype(F32)
    acts[2, pl.ds(0, length)] = gprod[pl.ds(0, length)] * fv[1].astype(F32)
    acts[1, pl.ds(length, 2)] = gprod[pl.ds(length, 2)] * kvh[1, pl.ds(0, 2)].astype(F32)
    acts[2, pl.ds(length, 2)] = gprod[pl.ds(length, 2)] * kvh[0, pl.ds(0, 2)].astype(F32)
    short(1)
    short(2)

    local[7].wait()

    def own_part(dest):
        at = pl.ds(pl.multiple_of(dest * length, length), length)
        y = lax.dot_general(iwv[0, at], gp[0], NT, preferred_element_type=F32)
        y = y + lax.dot_general(iwv[1, at], gp[1], NT, preferred_element_type=F32)
        y = y + lax.dot_general(iwv[2, at], gp[2], NT, preferred_element_type=F32)
        part[dest] = y

    def rs(d, q, slot):
        return remote(tx.at[d, q, slot], rx.at[d, q, slot], rs_s.at[d, q, slot],
                      rs_r.at[d, q, slot], chan=sides[d])

    def rs_send(d, q, slot, dest, half, before):
        y = part[dest, rows(half)]
        if before is not None:
            rs(d, q, before).wait_recv()
            y = y + rx[d, q, before].astype(F32)
        tx[d, q, slot] = y.astype(BF16)
        send(rs(d, q, slot))

    def residue_sends():
        for k in range(1, n_ctx):
            dst = lax.rem(me + n_ctx - k, n_ctx)
            send(remote(rown, rin.at[me], r_s.at[k], r_r.at[me], ctx=dst))

    def ycopy(half):
        return remote(ysend.at[half], yrecv.at[half], rsy_s.at[half], rsy_r.at[half], chan=partner)

    for q in range(2):
        owner = 1 - yh if q == 0 else yh
        far = chan_of(z + 4, owner)
        own_part(far)
        for d in range(2):
            rs_send(d, q, 0, far, d, None)
        near = {}
        for h in (3, 2, 1):
            for d in range(2):
                near[d, h] = chan_of(z + dirs[d] * h, owner)
                own_part(near[d, h])
            for late in range(2):
                for d in range(2):
                    half = d if late else 1 - d
                    slot = 1 + 2 * (3 - h) + late
                    if h == 3:
                        before = 0 if late else None
                    else:
                        before = slot - 2
                    rs_send(d, q, slot, near[d, h], half, before)
            if q == 0 and h == 3:
                residue_sends()
        mine = chan_of(z, owner)
        own_part(mine)
        for late in range(2):
            for d in range(2):
                rs(d, q, 5 + late).wait_recv()
        for half in range(2):
            y = part[mine, rows(half)]
            y = y + rx[0, q, 6 if half == 0 else 5].astype(F32)
            y = y + rx[1, q, 5 if half == 0 else 6].astype(F32)
            if q == 0:
                ysend[half] = y.astype(BF16)
                send(ycopy(half))
            else:
                ycopy(half).wait_recv()
                out[rows(half)] = (y + yrecv[half].astype(F32)).astype(BF16)

    rin[me] = rown[...]
    for k in range(1, n_ctx):
        src = lax.rem(me + k, n_ctx)
        remote(rown, rin.at[src], r_s.at[0], r_r.at[src], ctx=src).wait_recv()
    y = rin[0]
    for j in range(1, n_ctx):
        y = y + rin[j]
    gres[...] = y / (length * n_ctx)

    for c in sent:
        c.wait_send()
    for k in range(1, n_ctx):
        @pl.when(me >= k)
        def _():
            dst = lax.rem(me + n_ctx - k, n_ctx)
            remote(sown, sin.at[me], s_s.at[k], s_r.at[me], ctx=dst).wait_send()

    @pl.when(me > 0)
    def _():
        remote(hsend, hrecv, h_s.at[0], h_r.at[0], ctx=prev).wait_send()
        remote(feat.at[pl.ds(1, 2), pl.ds(0, 16)], kvh, kv_s.at[0], kv_r.at[0], ctx=prev).wait_send()


def local(features, saved_conv, grad_out, out_weight, in_weight, short_taps, residues, decay_time):
    length, width = grad_out.shape
    modes = residues.shape[0]
    n_chan = lax.axis_size("chan")
    n_ctx = lax.axis_size("ctx")
    half = length // 2
    dma = pltpu.SemaphoreType.DMA
    any_spec = pl.BlockSpec(memory_space=pl.ANY)
    vmem = pl.BlockSpec(memory_space=pltpu.VMEM)
    scratch = [
        pltpu.VMEM((n_chan, length, width), BF16),
        pltpu.VMEM(out_weight.shape, BF16),
        pltpu.VMEM(in_weight.shape, BF16),
        pltpu.VMEM(features.shape, BF16),
        pltpu.VMEM((length, width), BF16),
        pltpu.VMEM(short_taps.shape, F32),
        pltpu.VMEM((modes, width), F32),
        pltpu.VMEM((modes, width), F32),
        pltpu.VMEM((length, width), F32),
        pltpu.VMEM((length, width), F32),
        pltpu.VMEM((length, width), F32),
        pltpu.VMEM((3, length + 8, width), F32),
        pltpu.VMEM((3, length, width), BF16),
        pltpu.VMEM((length + 8, width), F32),
        pltpu.VMEM((4, modes, width), F32),
        pltpu.VMEM((modes, width), F32),
        pltpu.VMEM((CHAINS, modes, width), F32),
        pltpu.VMEM((modes, width), F32),
        pltpu.VMEM((n_ctx, modes, width), F32),
        pltpu.VMEM((16, width), F32),
        pltpu.VMEM((16, width), F32),
        pltpu.VMEM((2, 16, width), BF16),
        pltpu.VMEM((modes, width), F32),
        pltpu.VMEM((n_ctx, modes, width), F32),
        pltpu.VMEM((n_chan, length, width), F32),
        pltpu.VMEM((2, 2, 7, half, width), BF16),
        pltpu.VMEM((2, 2, 7, half, width), BF16),
        pltpu.VMEM((2, half, width), BF16),
        pltpu.VMEM((2, half, width), BF16),
        dma((8,)), dma((2, 2, 7)), dma((2, 2, 7)), dma((2,)), dma((2,)),
        dma((1,)), dma((1,)), dma((1,)), dma((1,)),
        dma((n_ctx,)), dma((n_ctx,)), dma((n_ctx,)), dma((n_ctx,)),
        dma((2, 2, 7)), dma((2, 2, 7)), dma((2,)), dma((2,)),
    ]
    return pl.pallas_call(
        kernel,
        out_shape=(
            jax.ShapeDtypeStruct((length, width), BF16),
            jax.ShapeDtypeStruct((modes, width), F32),
        ),
        in_specs=[any_spec] * 8,
        out_specs=(vmem, vmem),
        scratch_shapes=scratch,
        compiler_params=pltpu.CompilerParams(
            collective_id=0, has_side_effects=True, vmem_limit_bytes=48 * 1024 * 1024
        ),
    )(grad_out, features, saved_conv, out_weight, in_weight, short_taps, residues, decay_time)


def solution(mesh):
    return jax.shard_map(
        local,
        mesh=mesh,
        in_specs=(
            P(None, "ctx", "chan"),
            P("ctx", "chan"),
            P("ctx", "chan"),
            P("chan", None),
            P(None, None, "chan"),
            P(None, None, "chan"),
            P(None, "chan"),
            P(None, "chan"),
        ),
        out_specs=(P("chan", "ctx"), P(None, "chan")),
        check_vma=False,
    )
```

time: 451 us -> 92.1 us (0.20)
  waiting for transfers between devices: 303 us -> 0 us
  Pallas kernels: 0 us -> 82.5 us
  blocking collectives: 69.7 us -> 0 us
  starting transfers between devices: 20.6 us -> 0 us
  other arithmetic: 20.2 us -> 0 us
  between operations: 14.3 us -> 0.66 us
  matrix products: 10.5 us -> 0 us
    reduce_scatter x1 -> x0, waiting for transfers between devices: 154 us -> none  [local(): lax.psum_scatter(jnp.einsum('jdc,jtc->dt', in_weight, grad_proj, preferre...]
    all_gather x1 -> x0, waiting for transfers between devices: 82.5 us -> none  [local(): everything = lax.all_gather(grad_out, 'chan', axis=1, tiled=True)]
    pallas_call x0 -> x1, Pallas kernels: none -> 82.5 us  [local(): pl.pallas_call(kernel, out_shape=(jax.ShapeDtypeStruct((length, width), B...]
    psum x1 -> x0, blocking collectives: 69.7 us -> none  [local(): lax.psum(partial_res, 'ctx') / (length * lax.axis_size('ctx'))]
    ppermute x16 -> x0, waiting for transfers between devices: 65.2 us -> none  [passed_along(): lax.ppermute(value, axis, [(source, source + steps) for source in range(l...]
    ppermute x16 -> x0, starting transfers between devices: 20.5 us -> none  [passed_along(): lax.ppermute(value, axis, [(source, source + steps) for source in range(l...]
    dot_general x3 -> x0, matrix products: 10.5 us -> none  [the longest x1 6.03 us: local(): jnp.einsum('jdc,jtc->dt', in_weight, grad_proj, preferred_element_type=jn...]
    reduce_sum x3 -> x0, other arithmetic: 9.34 us -> none  [the longest x1 4.86 us: local(): jnp.sum(residues[None, None] * state, axis=2).reshape(length, width)]
  transfers between devices with their start and end apart: 18 -> 0, of which waited for: 18 -> 0; matrix products, arithmetic and copies ran while one was open for 3% -> 0% of each run, Pallas kernels for 0% -> 0%
where the time goes in v1:
time: 92.1 us; the launch traced here: 90.9 us
  Pallas kernels  82.5 us (90%)
  local copies, waits for them, and re-layouts  7.79 us (8%)
    pallas_call x1, Pallas kernels, local(): pl.pallas_call(kernel, out_shape=(jax.ShapeDtypeStruct((length, width), B...  82.5 us
    unnamed x16, local copies, waits for them, and re-layouts  7.79 us

profile of v1, /device:TPU:32, one launch (start us, length us, event | category | flops | bytes accessed | tf_op | source)
XLA Modules:
  0.0 90.9 jit_solution(2340916101967631282)
XLA Ops:
  0.6 0.0 copy-start
  0.6 1.6 %copy-done = bf16[256,4096]{1,0:T(8,128)(2,1)S(1)} copy-done((bf16[256,4096]{1,0:T(8,128)(2,1)S(1)}, bf16[256,4096]{1,0:T(8,128)(2,1)}, u32[]{:S(2)}) %copy-start) | copy-done | bytes 2097176
  2.2 0.0 copy-start.1
  2.2 1.0 %copy-done.1 = bf16[3,256,256]{2,1,0:T(8,128)(2,1)S(1)} copy-done((bf16[3,256,256]{2,1,0:T(8,128)(2,1)S(1)}, bf16[3,256,256]{2,1,0:T(8,128)(2,1)}, u32[]{:S(2)}) %copy-start.1) | copy-done | bytes 393240
  3.2 0.0 copy-start.2
  3.2 0.9 copy-done.2
  4.1 0.0 copy-start.3
  4.1 0.9 copy-done.3
  5.0 0.0 copy-start.4
  5.0 0.7 copy-done.4
  5.7 0.0 copy-start.5
  5.8 0.7 copy-done.5
  6.5 0.0 copy-start.6
  6.5 0.7 copy-done.6
  7.2 82.5 %shard_map.95 = (bf16[256,256]{1,0:T(8,128)(2,1)S(1)}, f32[16,256]{1,0:T(8,128)S(1)}) custom-call(bf16[256,256]{1,0:T(8,128)(2,1)S(1)} %copy-done.2, bf16[3,256,256]{2,1,0:T(8,128)(2,1)S(1)} %copy-done.1, bf16[256,256]{1,0:T(8,128)(2,1)S(1)} %copy-done.3, bf16[256,4096]{1,0:T(8,128)(2,1)S(1)} %copy-done, bf16[3,4096,256]{2,1,0:T(8,128)(2,1)} %iw.1, ...), custom_call_target="tpu_custom_call" | custom-call | tf_op jit(solution)/shard_map/pallas_call | solution.py:367
  89.7 0.7 copy.12
  90.3 0.6 copy.13
Async XLA Ops:
  0.6 1.6 %copy-start = (bf16[256,4096]{1,0:T(8,128)(2,1)S(1)}, bf16[256,4096]{1,0:T(8,128)(2,1)}, u32[]{:S(2)}) copy-start(bf16[256,4096]{1,0:T(8,128)(2,1)} %ow.1) | copy-start | bytes 6291460
  2.2 1.0 %copy-start.1 = (bf16[3,256,256]{2,1,0:T(8,128)(2,1)S(1)}, bf16[3,256,256]{2,1,0:T(8,128)(2,1)}, u32[]{:S(2)}) copy-start(bf16[3,256,256]{2,1,0:T(8,128)(2,1)} %feat.1) | copy-start | bytes 1179652
  3.2 0.9 copy-start.2
  4.1 0.9 copy-start.3
  5.0 0.7 copy-start.4
  5.7 0.7 copy-start.5
  6.5 0.7 copy-start.6

commit v2 on v1

v2 whole, which is shorter than its diff:
```python
import functools

import jax
import jax.numpy as jnp
from jax import lax
from jax.experimental import pallas as pl
from jax.experimental.pallas import tpu as pltpu
from jax.sharding import PartitionSpec as P

MESH = pl.DeviceIdType.MESH
F32 = jnp.float32
BF16 = jnp.bfloat16
NT = (((1,), (1,)), ((), ()))
CHAINS = 4

PIECES = 2
WIRE, HOP_Z, HOP_Y, AHEAD = 3.08 / PIECES, 1.7, 2.5, 1.6
CROSS = {1: (0, 1), 2: (), 3: (0, 1), 4: ()}
OFFSETS = (-3, -2, -1, 0, 1, 2, 3, 4)


def origin(item, link):
    plane, off, piece = item
    if link == "y":
        return (0, off, piece)
    if link == "+":
        return (plane, (off if off < 4 else -4) + 1, piece)
    return (plane, off - 1, piece)


def schedule():
    link = {}
    for plane in (0, 1):
        for off in OFFSETS:
            for piece in range(PIECES):
                if off == 0:
                    how = "y" if plane else "own"
                elif plane and piece in CROSS[abs(off)]:
                    how = "y"
                elif off == 4:
                    how = "+" if piece < PIECES // 2 else "-"
                else:
                    how = "+" if off < 0 else "-"
                link[plane, off, piece] = how
    kids = {item: [] for item in link}
    for item, how in link.items():
        if how != "own":
            kids[origin(item, how)].append(item)

    def hop(item):
        return HOP_Y if link[item] == "y" else HOP_Z

    def height(item):
        return max([WIRE + hop(k) + height(k) for k in kids[item]], default=0.0)

    free = {"+": 0.0, "-": 0.0, "y": 0.0}
    queue = {"+": [], "-": [], "y": []}
    pending = [(0.0, p, (0, 0, p)) for p in range(PIECES)]
    here, start, now, count = {}, {}, 0.0, PIECES
    while True:
        times = [p[0] for p in pending] + [max(free[c], now) for c in queue if queue[c]]
        if not times:
            break
        now = min(times)
        for entry in sorted(p for p in pending if p[0] <= now + 1e-9):
            pending.remove(entry)
            here[entry[2]] = entry[0]
            for k in kids[entry[2]]:
                queue[link[k]].append((-height(k), now, k))
        for c in queue:
            if queue[c] and free[c] <= now + 1e-9:
                queue[c].sort()
                k = queue[c].pop(0)[2]
                start[k], free[c] = now, now + WIRE
                pending.append((now + WIRE + hop(k), count, k))
                count += 1
    return link, kids, here, start


LINK, KIDS, HERE, START = schedule()
ITEMS = sorted(START)
INDEX = {item: i for i, item in enumerate(ITEMS)}
END = max(HERE.values())


def kernel(
    go, feat, conv, ow, iw, taps, res, decay,
    out, gres,
    blocks, owv, iwv, fv, cv, tv, rv, dv,
    acc, grow, prod, acts, gp, gprod, lam_ref, ent, csum,
    sown, sin, hsend, hrecv, kvh, rown, rin,
    part, tx, rx,
    in_sem, ag_s, ag_r, kv_s, kv_r, h_s, h_r,
    s_s, s_r, r_s, r_r, rs_s, rs_r,
):
    n_ctx = lax.axis_size("ctx")
    n_z = lax.axis_size("chan") // 2
    me = lax.axis_index("ctx")
    ch = lax.axis_index("chan")
    z = ch // 2
    yh = lax.rem(ch, 2)
    length = acc.shape[0]

    def chan_of(zz, yy):
        return lax.rem(zz + 2 * n_z, n_z) * 2 + yy

    partner = chan_of(z, 1 - yh)
    sides = [chan_of(z + 1, yh), chan_of(z - 1, yh)]

    pairs = [(go, blocks.at[ch]), (ow, owv), (feat, fv), (conv, cv), (taps, tv),
             (res, rv), (decay, dv), (iw, iwv)]
    local = [pltpu.make_async_copy(a, b, in_sem.at[i]) for i, (a, b) in enumerate(pairs)]
    for c in local:
        c.start()
    seen = set()

    def ready(*which):
        for i in which:
            if i not in seen:
                local[i].wait()
                seen.add(i)
    seen = set()

    def ready(*which):
        for i in which:
            if i not in seen:
                local[i].wait()
                seen.add(i)

    barrier = pltpu.get_barrier_semaphore()
    for dst in (sides[0], sides[1], partner):
        pl.semaphore_signal(barrier, inc=1, device_id={"chan": dst}, device_id_type=MESH)
    for k in range(1, n_ctx):
        pl.semaphore_signal(
            barrier, inc=1, device_id={"ctx": lax.rem(me + k, n_ctx)}, device_id_type=MESH
        )
    pl.semaphore_wait(barrier, 3 + n_ctx - 1)

    def remote(src, dst, ss, rs, **where):
        return pltpu.make_async_remote_copy(
            src_ref=src, dst_ref=dst, send_sem=ss, recv_sem=rs,
            device_id=where, device_id_type=MESH,
        )

    piece_rows = length // PIECES

    def rows(piece):
        return pl.ds(piece * piece_rows, piece_rows)

    def place(item):
        return chan_of(z + item[1], yh if item[0] == 0 else 1 - yh)

    onward = {"+": sides[0], "-": sides[1], "y": partner}
    back = {"+": sides[1], "-": sides[0], "y": partner}

    def ag(item, receiving=False):
        held = item if receiving else origin(item, LINK[item])
        ref = blocks.at[place(held), rows(item[2])]
        src = go.at[rows(item[2])] if LINK[held] == "own" else ref
        i = INDEX[item]
        return remote(src, ref, ag_s.at[i], ag_r.at[i], chan=onward[LINK[item]])

    sent = []
    guarded = []

    def finish():
        for c in sent:
            c.wait_send()
        for cond, c in guarded:
            pl.when(cond)(c.wait_send)

    def send_if(cond, c):
        pl.when(cond)(c.start)
        guarded.append((cond, c))

    def send(c):
        c.start()
        sent.append(c)

    steps = []
    for item in ITEMS:
        steps.append((max(HERE[origin(item, LINK[item])], START[item] - AHEAD), 1, item))
        steps.append((HERE[item], 0, item))
    steps.sort(key=lambda step: (step[0], step[1], START[step[2]]))
    head = [step for step in steps if step[1] == 1 and step[0] == 0.0]
    for _, _, item in head:
        send(ag(item))

    prev = lax.rem(me + n_ctx - 1, n_ctx)

    send_if(me > 0, remote(feat.at[pl.ds(1, 2), pl.ds(0, 16)], kvh, kv_s.at[0], kv_r.at[0], ctx=prev))

    @pl.when(me == n_ctx - 1)
    def _():
        kvh[...] = jnp.zeros_like(kvh)
        hrecv[...] = jnp.zeros_like(hrecv)

    first = [True]

    def multiply(block):
        cols = pl.ds(pl.multiple_of(block * length, length), length)
        term = lax.dot_general(blocks[block], owv[:, cols], NT, preferred_element_type=F32)
        if first[0]:
            acc[...] = term
            first[0] = False
        else:
            acc[...] += term

    ready(0, 1)
    multiply(ch)
    waiting = []
    arrived = {}
    prepared = False
    for when, kind, item in steps[len(head):]:
        if kind == 1:
            send(ag(item))
            continue
        ag(item, True).wait_recv()
        arrived[item[:2]] = arrived.get(item[:2], 0) + 1
        if waiting:
            multiply(place(waiting.pop(0) + (0,)))
        if arrived[item[:2]] == PIECES:
            waiting.append(item[:2])
        if not prepared and len(arrived) > 2:
            prepared = True
            ready(2, 3, 4, 5, 6)
            rate = 1.0 / dv[...]
            lam_ref[0] = jnp.exp(-rate)
            lam_ref[1] = jnp.exp(-rate * (length // CHAINS))
            lam_ref[2] = jnp.exp(-rate * length)
            lam_ref[3] = jnp.exp(rate)
            prod[...] = fv[1].astype(F32) * fv[2].astype(F32)
    for block in waiting:
        multiply(place(block + (0,)))

    gate = acc[...]
    grow[...] = gate * fv[0].astype(F32)
    acts[0, pl.ds(0, length)] = gate * cv[...].astype(F32)

    @pl.when(me > 0)
    def _():
        hsend[pl.ds(0, 8)] = acts[0, pl.ds(0, 8)]
        hsend[pl.ds(8, 8)] = grow[pl.ds(0, 8)]

    send_if(me > 0, remote(hsend, hrecv, h_s.at[0], h_r.at[0], ctx=prev))

    run = length // CHAINS
    lam = lam_ref[0]

    def sum_step(i, carry):
        fresh = []
        for k in range(CHAINS):
            g = grow[pl.ds(k * run + run - 1 - i, 1)]
            fresh.append(g + lam * carry[k])
        return tuple(fresh)

    zero = jnp.zeros_like(lam)
    sums = lax.fori_loop(0, run, sum_step, (zero,) * CHAINS, unroll=8)
    total = sums[CHAINS - 1]
    for k in range(CHAINS - 2, -1, -1):
        total = sums[k] + lam_ref[1] * total
    for k in range(CHAINS):
        csum[k] = sums[k]
    sown[...] = total

    for k in range(1, n_ctx):
        dst = lax.rem(me + n_ctx - k, n_ctx)
        send_if(me >= k, remote(sown, sin.at[me], s_s.at[k], s_r.at[me], ctx=dst))

    @pl.when(me < n_ctx - 1)
    def _():
        nxt = lax.rem(me + 1, n_ctx)
        remote(hsend, hrecv, h_s.at[0], h_r.at[0], ctx=nxt).wait_recv()
        remote(feat.at[pl.ds(1, 2), pl.ds(0, 16)], kvh, kv_s.at[0], kv_r.at[0], ctx=nxt).wait_recv()

    acts[0, pl.ds(length, 8)] = hrecv[pl.ds(0, 8)]

    def short(i):
        y = tv[i, pl.ds(0, 1)] * acts[i, pl.ds(0, length)]
        y = y + tv[i, pl.ds(1, 1)] * acts[i, pl.ds(1, length)]
        y = y + tv[i, pl.ds(2, 1)] * acts[i, pl.ds(2, length)]
        gp[i] = y.astype(BF16)

    short(0)

    ent[...] = jnp.zeros_like(ent)
    for j in range(n_ctx - 1, 0, -1):
        @pl.when(j > me)
        def _():
            remote(sown, sin.at[j], s_s.at[0], s_r.at[j], ctx=j).wait_recv()
            ent[...] = sin[j] + lam_ref[2] * ent[...]

    entering = ent[...]
    residue = rv[...]
    starts = [None] * CHAINS
    starts[CHAINS - 1] = entering
    for k in range(CHAINS - 2, -1, -1):
        starts[k] = csum[k + 1] + lam_ref[1] * starts[k + 1]

    def full_step(i, carry):
        states, totals = carry
        fresh, summed = [], []
        for k in range(CHAINS):
            r = k * run + run - 1 - i
            s = grow[pl.ds(r, 1)] + lam * states[k]
            gprod[pl.ds(r, 1)] = jnp.sum(residue * s, axis=0, keepdims=True)
            totals = totals + prod[pl.ds(r, 1)] * s
            fresh.append(s)
        return tuple(fresh), totals

    _, totals = lax.fori_loop(0, run, full_step, (tuple(starts), zero), unroll=4)
    rown[...] = totals
    beyond = (entering - hrecv[pl.ds(8, 1)]) * lam_ref[3]
    gprod[pl.ds(length, 1)] = jnp.sum(residue * entering, axis=0, keepdims=True)
    gprod[pl.ds(length + 1, 1)] = jnp.sum(residue * beyond, axis=0, keepdims=True)
    acts[1, pl.ds(0, length)] = gprod[pl.ds(0, length)] * fv[2].astype(F32)
    acts[2, pl.ds(0, length)] = gprod[pl.ds(0, length)] * fv[1].astype(F32)
    acts[1, pl.ds(length, 2)] = gprod[pl.ds(length, 2)] * kvh[1, pl.ds(0, 2)].astype(F32)
    acts[2, pl.ds(length, 2)] = gprod[pl.ds(length, 2)] * kvh[0, pl.ds(0, 2)].astype(F32)
    short(1)
    short(2)

    ready(7)

    def own_part(dest):
        at = pl.ds(pl.multiple_of(dest * length, length), length)
        y = lax.dot_general(iwv[0, at], gp[0], NT, preferred_element_type=F32)
        y = y + lax.dot_general(iwv[1, at], gp[1], NT, preferred_element_type=F32)
        y = y + lax.dot_general(iwv[2, at], gp[2], NT, preferred_element_type=F32)
        part[dest] = y

    def rs(item):
        i = INDEX[item]
        return remote(tx.at[i], rx.at[i], rs_s.at[i], rs_r.at[i], chan=back[LINK[item]])

    have = set()

    def summed(item):
        if item[:2] not in have:
            have.add(item[:2])
            own_part(place(item))
        y = part[place(item), rows(item[2])]
        for k in sorted(KIDS[item], key=lambda k: -START[k]):
            rs(k).wait_recv()
            y = y + rx[INDEX[k]].astype(F32)
        return y

    told = False
    for item in sorted(ITEMS, key=lambda item: (-HERE[item], -START[item])):
        if not told and END - HERE[item] > 4.0:
            told = True
            for k in range(1, n_ctx):
                dst = lax.rem(me + n_ctx - k, n_ctx)
                send(remote(rown, rin.at[me], r_s.at[k], r_r.at[me], ctx=dst))
        tx[INDEX[item]] = summed(item).astype(BF16)
        send(rs(item))
    for piece in range(PIECES):
        out[rows(piece)] = summed((0, 0, piece)).astype(BF16)

    rin[me] = rown[...]
    for k in range(1, n_ctx):
        src = lax.rem(me + k, n_ctx)
        remote(rown, rin.at[src], r_s.at[0], r_r.at[src], ctx=src).wait_recv()
    y = rin[0]
    for j in range(1, n_ctx):
        y = y + rin[j]
    gres[...] = y / (length * n_ctx)
    finish()


def local(features, saved_conv, grad_out, out_weight, in_weight, short_taps, residues, decay_time):
    length, width = grad_out.shape
    modes = residues.shape[0]
    n_chan = lax.axis_size("chan")
    n_ctx = lax.axis_size("ctx")
    dma = pltpu.SemaphoreType.DMA
    any_spec = pl.BlockSpec(memory_space=pl.ANY)
    vmem = pl.BlockSpec(memory_space=pltpu.VMEM)
    scratch = [
        pltpu.VMEM((n_chan, length, width), BF16),
        pltpu.VMEM(out_weight.shape, BF16),
        pltpu.VMEM(in_weight.shape, BF16),
        pltpu.VMEM(features.shape, BF16),
        pltpu.VMEM((length, width), BF16),
        pltpu.VMEM(short_taps.shape, F32),
        pltpu.VMEM((modes, width), F32),
        pltpu.VMEM((modes, width), F32),
        pltpu.VMEM((length, width), F32),
        pltpu.VMEM((length, width), F32),
        pltpu.VMEM((length, width), F32),
        pltpu.VMEM((3, length + 8, width), F32),
        pltpu.VMEM((3, length, width), BF16),
        pltpu.VMEM((length + 8, width), F32),
        pltpu.VMEM((4, modes, width), F32),
        pltpu.VMEM((modes, width), F32),
        pltpu.VMEM((CHAINS, modes, width), F32),
        pltpu.VMEM((modes, width), F32),
        pltpu.VMEM((n_ctx, modes, width), F32),
        pltpu.VMEM((16, width), F32),
        pltpu.VMEM((16, width), F32),
        pltpu.VMEM((2, 16, width), BF16),
        pltpu.VMEM((modes, width), F32),
        pltpu.VMEM((n_ctx, modes, width), F32),
        pltpu.VMEM((n_chan, length, width), F32),
        pltpu.VMEM((len(ITEMS), length // PIECES, width), BF16),
        pltpu.VMEM((len(ITEMS), length // PIECES, width), BF16),
        dma((8,)), dma((len(ITEMS),)), dma((len(ITEMS),)),
        dma((1,)), dma((1,)), dma((1,)), dma((1,)),
        dma((n_ctx,)), dma((n_ctx,)), dma((n_ctx,)), dma((n_ctx,)),
        dma((len(ITEMS),)), dma((len(ITEMS),)),
    ]
    return pl.pallas_call(
        kernel,
        out_shape=(
            jax.ShapeDtypeStruct((length, width), BF16),
            jax.ShapeDtypeStruct((modes, width), F32),
        ),
        in_specs=[any_spec] * 8,
        out_specs=(vmem, vmem),
        scratch_shapes=scratch,
        compiler_params=pltpu.CompilerParams(
            collective_id=0, has_side_effects=True, vmem_limit_bytes=67043328
        ),
    )(grad_out, features, saved_conv, out_weight, in_weight, short_taps, residues, decay_time)


def solution(mesh):
    return jax.shard_map(
        local,
        mesh=mesh,
        in_specs=(
            P(None, "ctx", "chan"),
            P("ctx", "chan"),
            P("ctx", "chan"),
            P("chan", None),
            P(None, None, "chan"),
            P(None, None, "chan"),
            P(None, "chan"),
            P(None, "chan"),
        ),
        out_specs=(P("chan", "ctx"), P(None, "chan")),
        check_vma=False,
    )
```

time: 92.1 us -> 68.8 us (0.75)
  Pallas kernels: 82.5 us -> 64.2 us
  local copies, waits for them, and re-layouts: 7.79 us -> 2.89 us
    pallas_call x1, Pallas kernels: 82.5 us -> 64.2 us  [local(): pl.pallas_call(kernel, out_shape=(jax.ShapeDtypeStruct((length, width), B...]
    unnamed x16 -> x2, local copies, waits for them, and re-layouts: 7.79 us -> 2.89 us
where the time goes in v2:
time: 68.8 us; the launch traced here: 67.8 us
  Pallas kernels  64.2 us (93%)
  local copies, waits for them, and re-layouts  2.89 us (4%)
    pallas_call x1, Pallas kernels, local(): pl.pallas_call(kernel, out_shape=(jax.ShapeDtypeStruct((length, width), B...  64.2 us
    unnamed x2, local copies, waits for them, and re-layouts  2.89 us

profile of v2, /device:TPU:32, one launch (start us, length us, event | category | flops | bytes accessed | tf_op | source)
XLA Modules:
  0.0 67.8 jit_solution(14214099565097125288)
XLA Ops:
  0.6 64.2 %shard_map.95 = (bf16[256,256]{1,0:T(8,128)(2,1)}, f32[16,256]{1,0:T(8,128)}) custom-call(bf16[256,256]{1,0:T(8,128)(2,1)} %go.1, bf16[3,256,256]{2,1,0:T(8,128)(2,1)} %feat.1, bf16[256,256]{1,0:T(8,128)(2,1)} %conv.1, bf16[256,4096]{1,0:T(8,128)(2,1)} %ow.1, bf16[3,4096,256]{2,1,0:T(8,128)(2,1)} %iw.1, f32[3,3,256]{2,1,0:T(4,128)} %taps.1, f32[16,256]{1,0:T(8,128)} %res.1, ...), custom_call_target="tpu_custom_call" | custom-call | tf_op jit(solution)/shard_map/pallas_call | solution.py:412
  64.9 1.6 %copy.12 = bf16[256,256]{1,0:T(8,128)(2,1)} copy(bf16[256,256]{1,0:T(8,128)(2,1)} %get-tuple-element.4) | data formatting | bytes 262144
  66.5 1.3 %copy.13 = f32[16,256]{1,0:T(8,128)} copy(f32[16,256]{1,0:T(8,128)} %get-tuple-element.5) | data formatting | bytes 32768

commit v3 on v2

--- a/solution.py
+++ b/solution.py
@@ -13,9 +13,9 @@
 NT = (((1,), (1,)), ((), ()))
 CHAINS = 4
 
-PIECES = 2
-WIRE, HOP_Z, HOP_Y, AHEAD = 3.08 / PIECES, 1.7, 2.5, 1.6
-CROSS = {1: (0, 1), 2: (), 3: (0, 1), 4: ()}
+PIECES = 4
+WIRE, HOP_Z, HOP_Y, AHEAD = 3.08 / PIECES, 2.2, 3.5, 1.6
+CROSS = {1: (0, 1), 2: (0, 1, 2), 3: (0, 1), 4: ()}
 OFFSETS = (-3, -2, -1, 0, 1, 2, 3, 4)
 
 
@@ -81,6 +81,7 @@
 ITEMS = sorted(START)
 INDEX = {item: i for i, item in enumerate(ITEMS)}
 END = max(HERE.values())
+HALFWAY = sorted(ITEMS, key=lambda item: HERE[item])[len(ITEMS) // 2]
 
 
 def kernel(
@@ -110,8 +111,7 @@
     pairs = [(go, blocks.at[ch]), (ow, owv), (feat, fv), (conv, cv), (taps, tv),
              (res, rv), (decay, dv), (iw, iwv)]
     local = [pltpu.make_async_copy(a, b, in_sem.at[i]) for i, (a, b) in enumerate(pairs)]
-    for c in local:
-        c.start()
+    local[0].start()
     seen = set()
 
     def ready(*which):
@@ -134,6 +134,7 @@
         pl.semaphore_signal(
             barrier, inc=1, device_id={"ctx": lax.rem(me + k, n_ctx)}, device_id_type=MESH
         )
+    ready(0)
     pl.semaphore_wait(barrier, 3 + n_ctx - 1)
 
     def remote(src, dst, ss, rs, **where):
@@ -156,9 +157,8 @@
     def ag(item, receiving=False):
         held = item if receiving else origin(item, LINK[item])
         ref = blocks.at[place(held), rows(item[2])]
-        src = go.at[rows(item[2])] if LINK[held] == "own" else ref
         i = INDEX[item]
-        return remote(src, ref, ag_s.at[i], ag_r.at[i], chan=onward[LINK[item]])
+        return remote(ref, ref, ag_s.at[i], ag_r.at[i], chan=onward[LINK[item]])
 
     sent = []
     guarded = []
@@ -185,6 +185,8 @@
     head = [step for step in steps if step[1] == 1 and step[0] == 0.0]
     for _, _, item in head:
         send(ag(item))
+    for c in local[1:7]:
+        c.start()
 
     prev = lax.rem(me + n_ctx - 1, n_ctx)
 
@@ -216,6 +218,8 @@
             send(ag(item))
             continue
         ag(item, True).wait_recv()
+        if item == HALFWAY:
+            local[7].start()
         arrived[item[:2]] = arrived.get(item[:2], 0) + 1
         if waiting:
             multiply(place(waiting.pop(0) + (0,)))

time: 68.8 us -> 64.8 us (0.942); the launches traced: 67.8 us -> 64.5 us
  Pallas kernels: 64.2 us -> 60.9 us
    pallas_call x1, Pallas kernels: 64.2 us -> 60.9 us  [local(): pl.pallas_call(kernel, out_shape=(jax.ShapeDtypeStruct((length, width), B...]
where the time goes in v3:
time: 64.8 us; the launch traced here: 64.5 us
  Pallas kernels  60.9 us (94%)
  local copies, waits for them, and re-layouts  2.89 us (4%)
    pallas_call x1, Pallas kernels, local(): pl.pallas_call(kernel, out_shape=(jax.ShapeDtypeStruct((length, width), B...  60.9 us
    unnamed x2, local copies, waits for them, and re-layouts  2.89 us

profile of v3, /device:TPU:32, one launch (start us, length us, event | category | flops | bytes accessed | tf_op | source)
XLA Modules:
  0.0 64.5 jit_solution(17362746805097083166)
XLA Ops:
  0.6 60.9 %shard_map.95 = (bf16[256,256]{1,0:T(8,128)(2,1)}, f32[16,256]{1,0:T(8,128)}) custom-call(bf16[256,256]{1,0:T(8,128)(2,1)} %go.1, bf16[3,256,256]{2,1,0:T(8,128)(2,1)} %feat.1, bf16[256,256]{1,0:T(8,128)(2,1)} %conv.1, bf16[256,4096]{1,0:T(8,128)(2,1)} %ow.1, bf16[3,4096,256]{2,1,0:T(8,128)(2,1)} %iw.1, f32[3,3,256]{2,1,0:T(4,128)} %taps.1, f32[16,256]{1,0:T(8,128)} %res.1, ...), custom_call_target="tpu_custom_call" | custom-call | tf_op jit(solution)/shard_map/pallas_call | solution.py:416
  61.6 1.6 %copy.12 = bf16[256,256]{1,0:T(8,128)(2,1)} copy(bf16[256,256]{1,0:T(8,128)(2,1)} %get-tuple-element.4) | data formatting | bytes 262144
  63.1 1.3 %copy.13 = f32[16,256]{1,0:T(8,128)} copy(f32[16,256]{1,0:T(8,128)} %get-tuple-element.5) | data formatting | bytes 32768

commit v4 on v3

--- a/solution.py
+++ b/solution.py
@@ -265,7 +265,7 @@
         total = sums[k] + lam_ref[1] * total
     for k in range(CHAINS):
         csum[k] = sums[k]
-    sown[...] = total
+    sown[...] = total.astype(BF16)
 
     for k in range(1, n_ctx):
         dst = lax.rem(me + n_ctx - k, n_ctx)
@@ -292,7 +292,7 @@
         @pl.when(j > me)
         def _():
             remote(sown, sin.at[j], s_s.at[0], s_r.at[j], ctx=j).wait_recv()
-            ent[...] = sin[j] + lam_ref[2] * ent[...]
+            ent[...] = sin[j].astype(F32) + lam_ref[2] * ent[...]
 
     entering = ent[...]
     residue = rv[...]
@@ -398,8 +398,8 @@
         pltpu.VMEM((4, modes, width), F32),
         pltpu.VMEM((modes, width), F32),
         pltpu.VMEM((CHAINS, modes, width), F32),
-        pltpu.VMEM((modes, width), F32),
-        pltpu.VMEM((n_ctx, modes, width), F32),
+        pltpu.VMEM((modes, width), BF16),
+        pltpu.VMEM((n_ctx, modes, width), BF16),
         pltpu.VMEM((16, width), F32),
         pltpu.VMEM((16, width), F32),
         pltpu.VMEM((2, 16, width), BF16),

time: 64.8 us -> 63.7 us (0.983)
  Pallas kernels: 60.9 us -> 60 us
    pallas_call x1, Pallas kernels: 60.9 us -> 60 us  [local(): pl.pallas_call(kernel, out_shape=(jax.ShapeDtypeStruct((length, width), B...]
where the time goes in v4:
time: 63.7 us; the launch traced here: 63.5 us
  Pallas kernels  60 us (94%)
  local copies, waits for them, and re-layouts  2.89 us (5%)
  between operations  0.64 us (1%)
    pallas_call x1, Pallas kernels, local(): pl.pallas_call(kernel, out_shape=(jax.ShapeDtypeStruct((length, width), B...  60 us
    unnamed x2, local copies, waits for them, and re-layouts  2.89 us

profile of v4, /device:TPU:32, one launch (start us, length us, event | category | flops | bytes accessed | tf_op | source)
XLA Modules:
  0.0 63.5 jit_solution(5975948123297026080)
XLA Ops:
  0.6 60.0 %shard_map.95 = (bf16[256,256]{1,0:T(8,128)(2,1)}, f32[16,256]{1,0:T(8,128)}) custom-call(bf16[256,256]{1,0:T(8,128)(2,1)} %go.1, bf16[3,256,256]{2,1,0:T(8,128)(2,1)} %feat.1, bf16[256,256]{1,0:T(8,128)(2,1)} %conv.1, bf16[256,4096]{1,0:T(8,128)(2,1)} %ow.1, bf16[3,4096,256]{2,1,0:T(8,128)(2,1)} %iw.1, f32[3,3,256]{2,1,0:T(4,128)} %taps.1, f32[16,256]{1,0:T(8,128)} %res.1, ...), custom_call_target="tpu_custom_call" | custom-call | tf_op jit(solution)/shard_map/pallas_call | solution.py:416
  60.6 1.6 %copy.12 = bf16[256,256]{1,0:T(8,128)(2,1)} copy(bf16[256,256]{1,0:T(8,128)(2,1)} %get-tuple-element.4) | data formatting | bytes 262144
  62.2 1.3 %copy.13 = f32[16,256]{1,0:T(8,128)} copy(f32[16,256]{1,0:T(8,128)} %get-tuple-element.5) | data formatting | bytes 32768
